TPU v7x, 32 devices: a whole 2x2x4 slice. The times are simulated.
32 devices in a mesh: groups: 1, leaf: 32 (over z, y, x, core).
Axes of the slice: x: 2, y: 2, z: 4, core: 2. Of those that a mesh axis runs over, the one named last changes fastest.
Arguments:
- embeddings: bfloat16 [768, 65536], P(None, ('groups', 'leaf')), may hold values from -4 to 4
- probes: bfloat16 [32, 65536], P(None, ('groups', 'leaf')), may hold values from -1.75 to 1.75
- order: int32 [32, 2048], P(('groups', 'leaf')), may hold values from 0 to 2047, each once within a row
- near_list: int32 [256, 7], P(('groups', 'leaf')), may hold values from 0 to 255, as said below
- near_count: int32 [32, 8], P(('groups', 'leaf')), may hold values from 1 to 7, 32 in all within a row
- skeleton: int32 [30, 64], P('groups'), may hold values from 0 to 65535, as said below
- core: float32 [30, 64, 64], P('groups'), may hold values from -8 to 8
Outputs:
- values: float32 [32, 65536], P(None, ('groups', 'leaf'))
Inputs may be any that keep to these rules, and one draw needn't show every extreme that they name: `near_list`: slot 0 of leaf t holds t; every slot of leaf t holds a leaf within 3 of t. `near_count`: each row sums to 32, and its largest entry is 7. `skeleton`: entry r of node n lies among the examples of node n, in the r-th of 64 equal parts of them. `order`: each row is a permutation.
All inputs are finite; a program needn't handle non-finite values.
Results may differ from a plain program's by a relative error of at most 0.0042.
Values may be sent and summed in bfloat16 or wider, within the bound.
No kernel may reach another device: no remote copies, remote signals or barrier semaphores. Data moves between devices by JAX's collectives and lax.ppermute only.
A program may use at most 128 MiB of HBM per device.

v0:
```python
import jax
import jax.numpy as jnp
from jax import lax
from jax.sharding import PartitionSpec as P

LEAF = 256
R = 64
LEVELS = 4
W = 3
NEAR = 7


def with_halo(block, sides, width):
    for axis, dim in sides:
        count = lax.axis_size(axis)
        forward = [(i, i + 1) for i in range(count - 1)]
        backward = [(target, source) for source, target in forward]
        low = lax.ppermute(
            lax.slice_in_dim(block, block.shape[dim] - width, None, axis=dim), axis, forward
        )
        high = lax.ppermute(lax.slice_in_dim(block, 0, width, axis=dim), axis, backward)
        block = jnp.concatenate([low, block, high], axis=dim)
    return block


def kernel_matrix(left_emb, left_norm, right_emb, right_norm):
    inner = lax.dot_general(
        left_emb, right_emb, (((0,), (0,)), ((), ())), preferred_element_type=jnp.float32
    )
    distance = left_norm[:, None] + right_norm[None, :] - 2.0 * inner
    return jnp.exp(-0.5 * distance).astype(jnp.bfloat16)


def leaf_kernels(source_emb, source_norm, target_emb, target_norm):
    inner = jnp.einsum("eia,eib->iab", source_emb, target_emb, preferred_element_type=jnp.float32)
    distance = source_norm[:, :, None] + target_norm[:, None, :] - 2.0 * inner
    return jnp.exp(-0.5 * distance).astype(jnp.bfloat16)


def column_norms(columns):
    return jnp.sum(jnp.square(columns.astype(jnp.float32)), axis=0)


def body(embeddings, probes, order, near_list, near_count, skeleton, core):
    axis_devices = lax.axis_size("leaf")
    tree_bits = axis_devices.bit_length() - 1
    position = lax.axis_index("leaf")
    width_e = embeddings.shape[0]
    dev_points = embeddings.shape[1]
    dev_leaves = dev_points // LEAF
    x_tree = probes[:, order[0]]
    probe_cols = x_tree.shape[0]
    norms = column_norms(embeddings)
    stacked = jnp.concatenate([embeddings, x_tree], axis=0)
    padded = with_halo(stacked, (("leaf", 1),), W * LEAF)
    pad_blocks = padded.reshape(padded.shape[0], dev_leaves + 2 * W, LEAF)
    pad_emb = pad_blocks[:width_e]
    pad_x = pad_blocks[width_e:]
    pad_norm = jnp.sum(jnp.square(pad_emb.astype(jnp.float32)), axis=0)
    own_emb = embeddings.reshape(width_e, dev_leaves, LEAF)
    own_norm = norms.reshape(dev_leaves, LEAF)
    local_pos = near_list - position * dev_leaves + W
    counts = near_count[0]
    near_sum = jnp.zeros((probe_cols, dev_leaves, LEAF), jnp.float32)
    for slot_id in range(NEAR):
        sources = local_pos[:, slot_id]
        kernel_vals = leaf_kernels(
            jnp.take(pad_emb, sources, axis=1),
            jnp.take(pad_norm, sources, axis=0),
            own_emb,
            own_norm,
        )
        terms = jnp.einsum(
            "pia,iab->pib",
            jnp.take(pad_x, sources, axis=1),
            kernel_vals,
            preferred_element_type=jnp.float32,
        )
        near_sum = near_sum + jnp.where((slot_id < counts)[None, :, None], terms, 0.0)
    level_bits = [tree_bits - 1 - level_id for level_id in range(LEVELS)]
    own_nodes = [
        2 ** (level_id + 1) - 2 + jnp.right_shift(position, level_bits[level_id])
        for level_id in range(LEVELS)
    ]
    partner_nodes = [
        2 ** (level_id + 1)
        - 2
        + jnp.bitwise_xor(jnp.right_shift(position, level_bits[level_id]), 1)
        for level_id in range(LEVELS)
    ]
    start_point = position * dev_points
    slot_counts = [R * 2 ** (level_id + 1) // axis_devices for level_id in range(LEVELS)]
    slot_starts = [sum(slot_counts[:level_id]) for level_id in range(LEVELS)]
    picks = []
    for level_id in range(LEVELS):
        node_row = lax.dynamic_index_in_dim(skeleton, own_nodes[level_id], 0, keepdims=False)
        within = jnp.bitwise_and(position, (1 << level_bits[level_id]) - 1)
        point_ids = lax.dynamic_slice_in_dim(
            node_row, within * slot_counts[level_id], slot_counts[level_id]
        )
        picks.append(jnp.take(embeddings, point_ids - start_point, axis=1))
    owned = jnp.concatenate(picks, axis=1)
    gathered = lax.all_gather(owned, "leaf", axis=1, tiled=True)
    gathered = gathered.reshape(width_e, axis_devices, owned.shape[1])
    own_parts = []
    part_parts = []
    for level_id in range(LEVELS):
        first_node = 2 ** (level_id + 1) - 2
        level_cols = gathered[
            :, :, slot_starts[level_id] : slot_starts[level_id] + slot_counts[level_id]
        ]
        level_cols = level_cols.reshape(width_e, axis_devices * slot_counts[level_id])
        own_parts.append(
            lax.dynamic_slice_in_dim(level_cols, (own_nodes[level_id] - first_node) * R, R, axis=1)
        )
        part_parts.append(
            lax.dynamic_slice_in_dim(
                level_cols, (partner_nodes[level_id] - first_node) * R, R, axis=1
            )
        )
    own_cols = jnp.concatenate(own_parts, axis=1)
    part_cols = jnp.concatenate(part_parts, axis=1)
    own_sums = jnp.dot(
        x_tree,
        kernel_matrix(embeddings, norms, own_cols, column_norms(own_cols)),
        preferred_element_type=jnp.float32,
    )
    node_terms = jnp.zeros((probe_cols, skeleton.shape[0] * R), jnp.float32)
    for level_id in range(LEVELS):
        node_terms = lax.dynamic_update_slice_in_dim(
            node_terms,
            own_sums[:, level_id * R : (level_id + 1) * R],
            own_nodes[level_id] * R,
            axis=1,
        )
    node_totals = lax.psum(node_terms, "leaf")
    partner_sums = [
        lax.dynamic_slice_in_dim(node_totals, partner_nodes[level_id] * R, R, axis=1)
        for level_id in range(LEVELS)
    ]
    weights = []
    for level_id in range(LEVELS):
        core_part = lax.dynamic_index_in_dim(core, partner_nodes[level_id], 0, keepdims=False)
        weights.append(
            jnp.dot(partner_sums[level_id], core_part, precision=lax.Precision.HIGHEST).astype(
                jnp.bfloat16
            )
        )
    far_kernel = kernel_matrix(part_cols, column_norms(part_cols), embeddings, norms)
    far_sum = jnp.dot(
        jnp.concatenate(weights, axis=1), far_kernel, preferred_element_type=jnp.float32
    )
    tree_values = near_sum.reshape(probe_cols, dev_points) + far_sum
    return jnp.zeros_like(tree_values).at[:, order[0]].set(tree_values)


def solution(mesh):
    return jax.shard_map(
        body,
        mesh=mesh,
        in_specs=(
            P(None, ("groups", "leaf")),
            P(None, ("groups", "leaf")),
            P(("groups", "leaf"), None),
            P(("groups", "leaf"), None),
            P(("groups", "leaf"), None),
            P("groups", None),
            P("groups", None, None),
        ),
        out_specs=P(None, ("groups", "leaf")),
        check_vma=False,
    )
```

profile of v0, /device:TPU:0, one launch (start us, length us, event | category | flops | bytes accessed | tf_op | source)
XLA Modules:
  0.0 336.7 jit_solution(11105078149921155437)
XLA Ops:
  6.5 0.9 compare_and_fusion.8
  7.4 0.8 compare_and_fusion.7
  8.2 0.8 compare_and_fusion.10
  9.0 0.7 subtract_add_fusion
  10.0 0.8 compare_and_fusion.9
  10.7 4.6 %copy.41 = bf16[768,2048]{0,1:T(8,128)(2,1)} copy(bf16[768,2048]{1,0:T(8,128)(2,1)} %param.13) | data formatting | bytes 6291456 | tf_op args[0]
  15.4 2.9 gather_fusion.1
  18.3 2.9 gather_fusion.2
  21.2 2.9 gather_fusion.3
  24.1 2.9 gather_fusion.4
  27.3 0.7 maximum_bitcast_fusion
  28.4 6.2 %gather_fusion = bf16[2048,32]{1,0:T(8,128)(2,1)S(1)} fusion(bf16[32,2048]{0,1:T(8,128)(2,1)S(1)} %copy.40, s32[2048]{0:T(1024)S(1)} %broadcast_clamp_fusion), kind=kCustom, calls=%fused_computation.21 | custom fusion | bytes 270336 | tf_op jit(solution)/shard_map/gather | solution.py:51
  34.6 3.0 pad_maximum_fusion.4
  37.6 2.5 copy.43
  40.1 1.4 collective-permute-start.1
  41.5 1.5 copy.42
  43.0 4.2 %collective-permute-start = (bf16[800,768]{1,0:T(8,128)(2,1)}, bf16[800,768]{1,0:T(8,128)(2,1)}, u32[]{:S(2)}, u32[]{:S(2)}) collective-permute-start(bf16[800,768]{1,0:T(8,128)(2,1)} %copy.42), channel_id=1, source_target_pairs={{0,1},{1,2},{2,3},{3,4},{4,5},{5,6},{6,7},{7,8},{8,9},{9,10},{10,1... | collective-permute-start | bytes 3686408 | tf_op jit(solution)/shard_map/ppermute | solution.py:18
  47.2 2.6 multiply_reduce_fusion.1
  50.1 1.8 copy.45
  51.9 2.5 copy.44
  54.3 6.6 %multiply_reduce_fusion = (f32[3584]{0:T(1024)S(1)}, bf16[768,3584]{0,1:T(8,128)(2,1)}) fusion(bf16[800,768]{0,1:T(8,128)(2,1)S(1)} %copy.45, bf16[32,2048]{0,1:T(8,128)(2,1)S(1)} %bitcast.279, bf16[768,2048]{0,1:T(8,128)(2,1)} %copy.41, bf16[800,768]{0,1:T(8,128)(2,1)} %copy.44), kind=kLoop, calls=%fused_computation.27 | loop fusion | flops 30274048 | bytes 11253760 | tf_op jit(solution)/shard_map/reduce_sum | solution.py:59
  61.0 2.1 pad_maximum_fusion.5
  63.1 1.5 copy.50
  64.6 0.6 gather_fusion.23
  65.1 0.6 gather_fusion.20
  65.7 0.6 gather_fusion.25
  66.8 0.6 gather_fusion.17
  67.9 0.6 gather_fusion.14
  69.1 0.6 gather_fusion.11
  69.6 0.6 gather_fusion.13
  70.2 0.6 gather_fusion.8
  71.3 0.6 gather_fusion.5
  72.5 8.2 %copy.46 = bf16[768,14,256]{2,0,1:T(8,128)(2,1)} copy(bf16[768,14,256]{0,2,1:T(8,128)(2,1)} %bitcast.269) | data formatting | bytes 11010048 | tf_op jit(solution)/shard_map/slice | solution.py:57
  80.7 5.1 %gather_fusion.6 = bf16[8,768,256]{2,1,0:T(8,128)(2,1)} fusion(bf16[768,14,256]{2,0,1:T(8,128)(2,1)} %copy.46, s32[1024]{0:T(1024)S(1)} %pad_clamp_fusion.10), kind=kCustom, calls=%fused_computation.1.clone | custom fusion | bytes 6291488 | tf_op jit(solution)/shard_map/jit(_take)/gather | solution.py:68
  85.7 5.0 %gather_fusion.9 = bf16[8,768,256]{2,1,0:T(8,128)(2,1)} fusion(bf16[768,14,256]{2,0,1:T(8,128)(2,1)} %copy.46, s32[1024]{0:T(1024)S(1)} %pad_clamp_fusion.9), kind=kCustom, calls=%fused_computation.9.clone | custom fusion | bytes 6291488 | tf_op jit(solution)/shard_map/jit(_take)/gather | solution.py:68
  90.7 5.0 %gather_fusion.12 = bf16[8,768,256]{2,1,0:T(8,128)(2,1)} fusion(bf16[768,14,256]{2,0,1:T(8,128)(2,1)} %copy.46, s32[1024]{0:T(1024)S(1)} %pad_clamp_fusion.8), kind=kCustom, calls=%fused_computation.10.clone | custom fusion | bytes 6291488 | tf_op jit(solution)/shard_map/jit(_take)/gather | solution.py:68
  95.6 5.0 %gather_fusion.15 = bf16[8,768,256]{2,1,0:T(8,128)(2,1)} fusion(bf16[768,14,256]{2,0,1:T(8,128)(2,1)} %copy.46, s32[1024]{0:T(1024)S(1)} %pad_clamp_fusion.7), kind=kCustom, calls=%fused_computation.11.clone | custom fusion | bytes 6291488 | tf_op jit(solution)/shard_map/jit(_take)/gather | solution.py:68
  100.6 5.0 %gather_fusion.18 = bf16[8,768,256]{2,1,0:T(8,128)(2,1)} fusion(bf16[768,14,256]{2,0,1:T(8,128)(2,1)} %copy.46, s32[1024]{0:T(1024)S(1)} %pad_clamp_fusion.6), kind=kCustom, calls=%fused_computation.12.clone | custom fusion | bytes 6291488 | tf_op jit(solution)/shard_map/jit(_take)/gather | solution.py:68
  105.7 5.1 %gather_fusion.21 = bf16[8,768,256]{2,1,0:T(8,128)(2,1)} fusion(bf16[768,14,256]{2,0,1:T(8,128)(2,1)} %copy.46, s32[1024]{0:T(1024)S(1)} %pad_clamp_fusion.5), kind=kCustom, calls=%fused_computation.13.clone | custom fusion | bytes 6291488 | tf_op jit(solution)/shard_map/jit(_take)/gather | solution.py:68
  110.8 5.0 %gather_fusion.24 = bf16[8,768,256]{2,1,0:T(8,128)(2,1)} fusion(bf16[768,14,256]{2,0,1:T(8,128)(2,1)} %copy.46, s32[1024]{0:T(1024)S(1)} %pad_clamp_fusion.4), kind=kCustom, calls=%fused_computation.14.clone | custom fusion | bytes 6291488 | tf_op jit(solution)/shard_map/jit(_take)/gather | solution.py:68
  116.2 3.9 %fusion.181 = f32[8,256,32]{1,2,0:T(8,128)S(1)} fusion(bf16[8,768,256]{2,1,0:T(8,128)(2,1)} %gather_fusion.6, pred[8]{0:T(512)(128)(4,1)S(1)} %get-tuple-element.58, f32[8,256]{1,0:T(8,128)S(1)} %add.373, f32[8,256]{1,0:T(8,128)S(1)} %broadcast_select_fusion.6, bf16[96,8,8,256]{3,2,1,0:T(8,128)(2,1)} %bitcast.270, ...), kind=kOutput, calls=%fused_computation.117 | convolution fusion | flops 843186176 | bytes 6701072 | tf_op jit(solution)/shard_map/pia,iab->pib/dot_general | solution.py:73
  120.1 3.9 %fusion.176 = f32[8,256,32]{1,2,0:T(8,128)S(1)} fusion(f32[8,256,32]{1,2,0:T(8,128)S(1)} %fusion.181, bf16[8,768,256]{2,1,0:T(8,128)(2,1)} %gather_fusion.9, pred[8]{0:T(512)(128)(4,1)S(1)} %get-tuple-element.57, f32[8,256]{1,0:T(8,128)S(1)} %broadcast_select_fusion.5, f32[8,256]{1,0:T(8,128)S(1)} %add.373, bf16[96,8,8,256]{3,2,1,0:T(8,128)(2,1)} %bitcast.271, ...), kind=kOutput, calls=%fused_computation.116 | convolution fusion | flops 843251712 | bytes 6963216 | tf_op jit(solution)/shard_map/pia,iab->pib/dot_general | solution.py:73
  124.0 3.9 %fusion.166 = f32[8,256,32]{1,2,0:T(8,128)S(1)} fusion(f32[8,256,32]{1,2,0:T(8,128)S(1)} %fusion.176, bf16[8,768,256]{2,1,0:T(8,128)(2,1)} %gather_fusion.12, pred[8]{0:T(512)(128)(4,1)S(1)} %get-tuple-element.56, f32[8,256]{1,0:T(8,128)S(1)} %broadcast_select_fusion.4, f32[8,256]{1,0:T(8,128)S(1)} %add.373, bf16[96,8,8,256]{3,2,1,0:T(8,128)(2,1)} %bitcast.272, ...), kind=kOutput, calls=%fused_computation.114 | convolution fusion | flops 843251712 | bytes 6963216 | tf_op jit(solution)/shard_map/pia,iab->pib/dot_general | solution.py:73
  127.9 3.9 %fusion.156 = f32[8,256,32]{1,2,0:T(8,128)S(1)} fusion(f32[8,256,32]{1,2,0:T(8,128)S(1)} %fusion.166, bf16[8,768,256]{2,1,0:T(8,128)(2,1)} %gather_fusion.15, pred[8]{0:T(512)(128)(4,1)S(1)} %get-tuple-element.55, f32[8,256]{1,0:T(8,128)S(1)} %broadcast_select_fusion.3, f32[8,256]{1,0:T(8,128)S(1)} %add.373, bf16[96,8,8,256]{3,2,1,0:T(8,128)(2,1)} %bitcast.273, ...), kind=kOutput, calls=%fused_computation.112 | convolution fusion | flops 843251712 | bytes 6963216 | tf_op jit(solution)/shard_map/pia,iab->pib/dot_general | solution.py:73
  131.8 3.9 %fusion.146 = f32[8,256,32]{1,2,0:T(8,128)S(1)} fusion(f32[8,256,32]{1,2,0:T(8,128)S(1)} %fusion.156, bf16[8,768,256]{2,1,0:T(8,128)(2,1)} %gather_fusion.18, pred[8]{0:T(512)(128)(4,1)S(1)} %get-tuple-element.54, f32[8,256]{1,0:T(8,128)S(1)} %broadcast_select_fusion.2, f32[8,256]{1,0:T(8,128)S(1)} %add.373, bf16[96,8,8,256]{3,2,1,0:T(8,128)(2,1)} %bitcast.274, ...), kind=kOutput, calls=%fused_computation.110 | convolution fusion | flops 843251712 | bytes 6963216 | tf_op jit(solution)/shard_map/pia,iab->pib/dot_general | solution.py:73
  135.7 5.2 %fusion.136 = f32[8,256,32]{1,2,0:T(8,128)} fusion(f32[8,256,32]{1,2,0:T(8,128)S(1)} %fusion.146, bf16[8,768,256]{2,1,0:T(8,128)(2,1)} %gather_fusion.21, pred[8]{0:T(512)(128)(4,1)S(1)} %get-tuple-element.53, f32[8,256]{1,0:T(8,128)S(1)} %broadcast_select_fusion.1, f32[8,256]{1,0:T(8,128)S(1)} %add.373, bf16[96,8,8,256]{3,2,1,0:T(8,128)(2,1)} %bitcast.275, ...), kind=kOutput, calls=%fused_computation.108 | convolution fusion | flops 843251712 | bytes 6963216 | tf_op jit(solution)/shard_map/pia,iab->pib/dot_general | solution.py:73
  140.9 5.3 %reshape.494 = bf16[1920,768]{1,0:T(8,128)(2,1)} reshape(bf16[32,60,768]{2,1,0:T(8,128)(2,1)} %all-gather.3.cloned.1.call-done) | data formatting | bytes 5898240
  146.2 5.3 %reshape.251 = bf16[768,32,60]{0,2,1:T(8,128)(2,1)} reshape(bf16[768,1920]{0,1:T(8,128)(2,1)} %bitcast.277) | data formatting | bytes 5898240 | tf_op jit(solution)/shard_map/reshape | solution.py:104
  151.5 1.0 slice.136
  152.6 1.3 slice_bitcast_fusion
  153.8 1.5 slice.138
  155.4 3.4 %slice.139 = bf16[768,32,32]{0,2,1:T(8,128)(2,1)} slice(bf16[768,32,60]{0,2,1:T(8,128)(2,1)} %reshape.251), slice={[0:768], [0:32], [28:60]} | slice | bytes 3145728 | tf_op jit(solution)/shard_map/slice | solution.py:109
  158.9 1.0 constant_dynamic-slice_fusion.4
  160.1 3.3 fusion.52
  165.0 0.7 copy-done.1
  165.7 3.9 %fusion.126 = f32[8,4,8,256]{3,2,1,0:T(8,128)S(1)} fusion(f32[8,256,32]{1,2,0:T(8,128)S(1)} %copy-done.5, bf16[8,768,256]{2,1,0:T(8,128)(2,1)} %gather_fusion.24, pred[8]{0:T(512)(128)(4,1)S(1)} %get-tuple-element.52, f32[8,256]{1,0:T(8,128)S(1)} %broadcast_select_fusion, f32[8,256]{1,0:T(8,128)S(1)} %add.373, bf16[96,8,8,256]{3,2,1,0:T(8,128)(2,1)} %bitcast.276, ...), kind=kOutput, calls=%fused_computation.106 | convolution fusion | flops 843251712 | bytes 6963216 | tf_op jit(solution)/shard_map/pia,iab->pib/dot_general | solution.py:73
  169.8 145.9 %all-reduce.2.cloned.1.call-done = f32[32,1920]{1,0:T(8,128)} async-done(((f32[32,1920]{1,0:T(8,128)}), f32[32,1920]{1,0:T(8,128)}) %all-reduce.2.cloned.1.call-update) | async-done | bytes 245776 | tf_op jit(solution)/shard_map/psum | solution.py:136
  315.7 0.9 convolution_convert_fusion
  316.6 0.9 convolution_convert_fusion.1
  317.6 0.9 convolution_convert_fusion.2
  318.5 0.9 convolution_convert_fusion.3
  319.4 3.2 fusion.44
  323.0 5.8 %scatter_custom_fusion = f32[32,2048]{0,1:T(8,128)S(1)} fusion(s32[2048]{0:T(1024)S(1)} %bitcast.286, f32[2048,32]{1,0:T(8,128)S(1)} %copy.80, f32[]{:T(128)} %constant.201.clone.1), kind=kCustom, calls=%fused_computation.168 | custom fusion | bytes 262148 | tf_op jit(solution)/shard_map/scatter | solution.py:154
  328.9 1.0 copy.81
  (77 shorter events, 6.7 us)
Async XLA Ops:
  6.5 309.1 %copy-start = (f32[30,64,64]{2,1,0:T(8,128)S(1)}, f32[30,64,64]{2,1,0:T(8,128)}, u32[]{:S(2)}) copy-start(f32[30,64,64]{2,1,0:T(8,128)} %param.19) | copy-start | bytes 1474564
  6.5 134.4 %all-gather.3.cloned.1.call-start = ((), (), s32[]{:S(2)}) async-start(), calls=%async_computation.1 | async-start | bytes 3244032 | tf_op jit(solution)/shard_map/all_gather | solution.py:103
  18.2 9.8 %copy-start.3 = (s32[1,2048]{1,0:T(1,128)S(1)}, s32[1,2048]{1,0:T(1,128)}, u32[]{:S(2)}) copy-start(s32[1,2048]{1,0:T(1,128)} %param.15) | copy-start | bytes 24580
  18.3 9.9 %copy-start.2 = (bf16[32,2048]{1,0:T(8,128)(2,1)S(1)}, bf16[32,2048]{1,0:T(8,128)(2,1)}, u32[]{:S(2)}) copy-start(bf16[32,2048]{1,0:T(8,128)(2,1)} %param.14) | copy-start | bytes 393220
  28.0 287.6 %all-reduce.2.cloned.1.call-start = ((), (), s32[]{:S(2)}) async-start(), calls=%async_computation | async-start | bytes 491520 | tf_op jit(solution)/shard_map/psum | solution.py:136
  40.1 9.9 %copy-start.4 = (s32[1,8]{1,0:T(1,128)S(1)}, s32[1,8]{1,0:T(1,128)}, u32[]{:S(2)}) copy-start(s32[1,8]{1,0:T(1,128)} %param.17) | copy-start | bytes 100
  40.1 10.0 %collective-permute-start.1 = (bf16[800,768]{1,0:T(8,128)(2,1)}, bf16[800,768]{1,0:T(8,128)(2,1)}, u32[]{:S(2)}, u32[]{:S(2)}) collective-permute-start(bf16[800,768]{1,0:T(8,128)(2,1)} %copy.43), channel_id=1, source_target_pairs={{1,0},{2,1},{3,2},{4,3},{5,4},{6,5},{7,6},{8,7},{9,8},{10,9},{11,1... | collective-permute-start | bytes 3686408 | tf_op jit(solution)/shard_map/ppermute | solution.py:21
  43.0 8.8 %collective-permute-start = (bf16[800,768]{1,0:T(8,128)(2,1)}, bf16[800,768]{1,0:T(8,128)(2,1)}, u32[]{:S(2)}, u32[]{:S(2)}) collective-permute-start(bf16[800,768]{1,0:T(8,128)(2,1)} %copy.42), channel_id=1, source_target_pairs={{0,1},{1,2},{2,3},{3,4},{4,5},{5,6},{6,7},{7,8},{8,9},{9,10},{10,1... | collective-permute-start | bytes 3686408 | tf_op jit(solution)/shard_map/ppermute | solution.py:18
  160.1 5.6 %copy-start.5 = (f32[8,256,32]{1,2,0:T(8,128)S(1)}, f32[8,256,32]{1,2,0:T(8,128)}, u32[]{:S(2)}) copy-start(f32[8,256,32]{1,2,0:T(8,128)} %fusion.136) | copy-start | bytes 786436
  165.0 0.7 copy-start.1
Sparse Core Ops, SparseCore 0:
  28.2 68.4 all-gather.2
  165.8 149.8 all-reduce.1
where the time goes:
time: 339 us; the launch traced here: 337 us
  waiting for transfers between devices  146 us (43%)
  local copies, waits for them, and re-layouts  112 us (33%)
  matrix products  38.8 us (11%)
  other arithmetic  20.1 us (6%)
  between operations  14 us (4%)
  starting transfers between devices  5.62 us (2%)
    psum x1, waiting for transfers between devices, body(): node_totals = lax.psum(node_terms, 'leaf')  146 us
    gather x7, local copies, waits for them, and re-layouts, body(): jnp.take(pad_emb, sources, axis=1)  35.1 us
    dot_general x7, matrix products, body(): jnp.einsum('pia,iab->pib', jnp.take(pad_x, sources, axis=1), kernel_vals,...  28.6 us
    gather x4, local copies, waits for them, and re-layouts, body(): picks.append(jnp.take(embeddings, point_ids - start_point, axis=1))  11.6 us
    unnamed x15, local copies, waits for them, and re-layouts  10.9 us
    slice x1, local copies, waits for them, and re-layouts, body(): pad_emb = pad_blocks[:width_e]  8.19 us
    scatter x2, local copies, waits for them, and re-layouts, body(): return jnp.zeros_like(tree_values).at[:, order[0]].set(tree_values)  6.86 us
  transfers between devices with their start and end apart: 4, of which 1 were waited for; matrix products, arithmetic and copies ran while one was open for 33% of the time, Pallas kernels for 0%

commit v1 on v0

--- a/solution.py
+++ b/solution.py
@@ -133,7 +133,8 @@
             own_nodes[level_id] * R,
             axis=1,
         )
-    node_totals = lax.psum(node_terms, "leaf")
+    pieces = lax.all_gather(node_terms, "leaf")
+    node_totals = jnp.sum(pieces, axis=0)
     partner_sums = [
         lax.dynamic_slice_in_dim(node_totals, partner_nodes[level_id] * R, R, axis=1)
         for level_id in range(LEVELS)

time: 339 us -> 277 us (0.82)
  the two profiles are of different devices: /device:TPU:0 before, /device:TPU:13 now
where the time goes in v1:
time: 277 us; the launch traced here: 275 us
  local copies, waits for them, and re-layouts  113 us (41%)
  waiting for transfers between devices  83.4 us (30%)
  matrix products  34.9 us (13%)
  other arithmetic  24.1 us (9%)
  between operations  14.2 us (5%)
  starting transfers between devices  5.77 us (2%)
    all_gather x1, waiting for transfers between devices, body(): gathered = lax.all_gather(owned, 'leaf', axis=1, tiled=True)  50.5 us
    gather x7, local copies, waits for them, and re-layouts, body(): jnp.take(pad_emb, sources, axis=1)  34.9 us
    ppermute x1, waiting for transfers between devices, with_halo(): lax.ppermute(lax.slice_in_dim(block, 0, width, axis=dim), axis, backward)  32.9 us
    dot_general x7, matrix products, body(): jnp.einsum('pia,iab->pib', jnp.take(pad_x, sources, axis=1), kernel_vals,...  27.5 us
    gather x4, local copies, waits for them, and re-layouts, body(): picks.append(jnp.take(embeddings, point_ids - start_point, axis=1))  11.6 us
    unnamed x23, local copies, waits for them, and re-layouts  11 us
    slice x1, local copies, waits for them, and re-layouts, body(): pad_emb = pad_blocks[:width_e]  8.29 us
    scatter x2, local copies, waits for them, and re-layouts, body(): return jnp.zeros_like(tree_values).at[:, order[0]].set(tree_values)  6.86 us
  transfers between devices with their start and end apart: 4, of which 2 were waited for; matrix products, arithmetic and copies ran while one was open for 40% of the time, Pallas kernels for 0%

profile of v1, /device:TPU:13, one launch (start us, length us, event | category | flops | bytes accessed | tf_op | source)
XLA Modules:
  0.0 275.3 jit_solution(9043692153368033709)
XLA Ops:
  6.5 0.9 compare_and_fusion.8
  7.4 0.8 compare_and_fusion.7
  8.2 0.8 compare_and_fusion.10
  9.0 0.7 subtract_add_fusion
  9.7 0.8 slice_reduce_fusion
  10.4 1.3 compare_and_fusion.9
  11.7 4.7 %copy.41 = bf16[768,2048]{0,1:T(8,128)(2,1)} copy(bf16[768,2048]{1,0:T(8,128)(2,1)} %param.13) | data formatting | bytes 6291456 | tf_op args[0]
  16.5 2.9 %gather_fusion.1 = bf16[4,768]{1,0:T(4,128)(2,1)S(1)} fusion(bf16[768,2048]{0,1:T(8,128)(2,1)} %copy.41, s32[1024]{0:T(1024)S(1)} %pad_clamp_fusion.3), kind=kCustom, calls=%fused_computation.22 | custom fusion | bytes 12304 | tf_op jit(solution)/shard_map/jit(_take)/gather | solution.py:101
  19.4 2.9 %gather_fusion.2 = bf16[8,768]{1,0:T(8,128)(2,1)S(1)} fusion(bf16[768,2048]{0,1:T(8,128)(2,1)} %copy.41, s32[1024]{0:T(1024)S(1)} %pad_clamp_fusion.2), kind=kCustom, calls=%fused_computation.23 | custom fusion | bytes 24608 | tf_op jit(solution)/shard_map/jit(_take)/gather | solution.py:101
  22.3 2.9 %gather_fusion.3 = bf16[16,768]{1,0:T(8,128)(2,1)S(1)} fusion(bf16[768,2048]{0,1:T(8,128)(2,1)} %copy.41, s32[1024]{0:T(1024)S(1)} %pad_clamp_fusion.1), kind=kCustom, calls=%fused_computation.24 | custom fusion | bytes 49216 | tf_op jit(solution)/shard_map/jit(_take)/gather | solution.py:101
  25.2 2.9 %gather_fusion.4 = bf16[32,768]{1,0:T(8,128)(2,1)S(1)} fusion(bf16[768,2048]{0,1:T(8,128)(2,1)} %copy.41, s32[1024]{0:T(1024)S(1)} %pad_clamp_fusion), kind=kCustom, calls=%fused_computation.25 | custom fusion | bytes 98432 | tf_op jit(solution)/shard_map/jit(_take)/gather | solution.py:101
  28.4 0.7 maximum_bitcast_fusion
  29.6 6.2 %gather_fusion = bf16[2048,32]{1,0:T(8,128)(2,1)S(1)} fusion(bf16[32,2048]{0,1:T(8,128)(2,1)S(1)} %copy.40, s32[2048]{0:T(1024)S(1)} %broadcast_clamp_fusion), kind=kCustom, calls=%fused_computation.21 | custom fusion | bytes 270336 | tf_op jit(solution)/shard_map/gather | solution.py:51
  35.8 2.6 multiply_reduce_fusion.1
  38.3 50.5 %all-gather.6.cloned.1.call-done = bf16[32,60,768]{2,1,0:T(8,128)(2,1)} async-done(((bf16[1,60,768]{2,1,0:T(8,128)(2,1)}), bf16[32,60,768]{2,1,0:T(8,128)(2,1)}) %all-gather.6.cloned.1.call-update) | async-done | bytes 2949136 | tf_op jit(solution)/shard_map/all_gather | solution.py:103
  88.8 5.3 %reshape.502 = bf16[1920,768]{1,0:T(8,128)(2,1)} reshape(bf16[32,60,768]{2,1,0:T(8,128)(2,1)} %all-gather.6.cloned.1.call-done) | data formatting | bytes 5898240
  94.1 5.3 %reshape.259 = bf16[768,32,60]{0,2,1:T(8,128)(2,1)} reshape(bf16[768,1920]{0,1:T(8,128)(2,1)} %bitcast.285) | data formatting | bytes 5898240 | tf_op jit(solution)/shard_map/reshape | solution.py:104
  99.4 1.0 slice.136
  100.5 1.3 slice_bitcast_fusion
  101.7 1.5 slice.138
  103.3 3.4 %slice.139 = bf16[768,32,32]{0,2,1:T(8,128)(2,1)} slice(bf16[768,32,60]{0,2,1:T(8,128)(2,1)} %reshape.259), slice={[0:768], [0:32], [28:60]} | slice | bytes 3145728 | tf_op jit(solution)/shard_map/slice | solution.py:109
  106.8 1.0 constant_dynamic-slice_fusion.4
  108.0 3.3 %fusion.52 = f32[32,256]{1,0:T(8,128)S(1)} fusion(bf16[2048,32]{1,0:T(8,128)(2,1)S(1)} %gather_fusion, bf16[768,2048]{1,0:T(8,128)(2,1)} %param.13, f32[256]{0:T(256)S(1)} %multiply_reduce_fusion.3, f32[2048]{0:T(1024)S(1)} %multiply_reduce_fusion.1, bf16[768,64]{0,1:T(8,128)(2,1)S(1)} %get-tuple-element.27, bf16[768,64]{0,1:T(8,128)(2,1)S(1)} %get-tuple-element.29, ...), kind=kOutput, calls=%fused_computation.96 | convolution fusion | flops 843055104 | bytes 3712000 | tf_op jit(solution)/shard_map/dot_general | solution.py:123
  113.0 0.7 copy-done.1
  113.7 2.9 %pad_maximum_fusion.4 = (bf16[800,768]{0,1:T(8,128)(2,1)S(1)}, bf16[800,768]{0,1:T(8,128)(2,1)}) fusion(bf16[32,2048]{0,1:T(8,128)(2,1)S(1)} %bitcast.286, bf16[768,2048]{0,1:T(8,128)(2,1)} %copy.41), kind=kLoop, calls=%fused_computation.95 | loop fusion | flops 4915200 | bytes 5734400 | tf_op jit(solution)/shard_map/slice | solution.py:19
  116.7 2.5 copy.43
  119.1 2.1 collective-permute-start.1
  121.3 1.5 copy.42
  122.8 3.6 %collective-permute-start = (bf16[800,768]{1,0:T(8,128)(2,1)}, bf16[800,768]{1,0:T(8,128)(2,1)}, u32[]{:S(2)}, u32[]{:S(2)}) collective-permute-start(bf16[800,768]{1,0:T(8,128)(2,1)} %copy.42), channel_id=1, source_target_pairs={{0,1},{1,2},{2,3},{3,4},{4,5},{5,6},{6,7},{7,8},{8,9},{9,10},{10,1... | collective-permute-start | bytes 3686408 | tf_op jit(solution)/shard_map/ppermute | solution.py:18
  126.7 32.9 %collective-permute-done.1 = bf16[800,768]{1,0:T(8,128)(2,1)} collective-permute-done((bf16[800,768]{1,0:T(8,128)(2,1)}, bf16[800,768]{1,0:T(8,128)(2,1)}, u32[]{:S(2)}, u32[]{:S(2)}) %collective-permute-start.1) | collective-permute-done | bytes 1228832 | tf_op jit(solution)/shard_map/ppermute | solution.py:21
  159.6 1.8 copy.45
  161.4 2.5 copy.44
  163.9 6.7 %multiply_reduce_fusion = (f32[3584]{0:T(1024)S(1)}, bf16[768,3584]{0,1:T(8,128)(2,1)}) fusion(bf16[800,768]{0,1:T(8,128)(2,1)S(1)} %copy.45, bf16[32,2048]{0,1:T(8,128)(2,1)S(1)} %bitcast.287, bf16[768,2048]{0,1:T(8,128)(2,1)} %copy.41, bf16[800,768]{0,1:T(8,128)(2,1)} %copy.44), kind=kLoop, calls=%fused_computation.27 | loop fusion | flops 30274048 | bytes 11253760 | tf_op jit(solution)/shard_map/reduce_sum | solution.py:59
  170.5 2.1 pad_maximum_fusion.5
  172.6 1.5 copy.50
  174.1 0.6 gather_fusion.23
  174.7 0.6 gather_fusion.20
  175.2 0.6 gather_fusion.25
  175.8 0.6 gather_fusion.22
  176.4 0.6 gather_fusion.17
  176.9 0.6 gather_fusion.19
  177.5 0.6 gather_fusion.14
  178.6 0.6 gather_fusion.11
  179.7 0.6 gather_fusion.8
  180.9 0.6 gather_fusion.5
  182.0 8.3 %copy.46 = bf16[768,14,256]{2,0,1:T(8,128)(2,1)} copy(bf16[768,14,256]{0,2,1:T(8,128)(2,1)} %bitcast.277) | data formatting | bytes 11010048 | tf_op jit(solution)/shard_map/slice | solution.py:57
  190.3 5.1 %gather_fusion.6 = bf16[8,768,256]{2,1,0:T(8,128)(2,1)} fusion(bf16[768,14,256]{2,0,1:T(8,128)(2,1)} %copy.46, s32[1024]{0:T(1024)S(1)} %pad_clamp_fusion.10), kind=kCustom, calls=%fused_computation.1.clone | custom fusion | bytes 6291488 | tf_op jit(solution)/shard_map/jit(_take)/gather | solution.py:68
  195.4 5.0 %gather_fusion.9 = bf16[8,768,256]{2,1,0:T(8,128)(2,1)} fusion(bf16[768,14,256]{2,0,1:T(8,128)(2,1)} %copy.46, s32[1024]{0:T(1024)S(1)} %pad_clamp_fusion.9), kind=kCustom, calls=%fused_computation.9.clone | custom fusion | bytes 6291488 | tf_op jit(solution)/shard_map/jit(_take)/gather | solution.py:68
  200.3 5.0 %gather_fusion.12 = bf16[8,768,256]{2,1,0:T(8,128)(2,1)} fusion(bf16[768,14,256]{2,0,1:T(8,128)(2,1)} %copy.46, s32[1024]{0:T(1024)S(1)} %pad_clamp_fusion.8), kind=kCustom, calls=%fused_computation.10.clone | custom fusion | bytes 6291488 | tf_op jit(solution)/shard_map/jit(_take)/gather | solution.py:68
  205.3 5.0 %gather_fusion.15 = bf16[8,768,256]{2,1,0:T(8,128)(2,1)} fusion(bf16[768,14,256]{2,0,1:T(8,128)(2,1)} %copy.46, s32[1024]{0:T(1024)S(1)} %pad_clamp_fusion.7), kind=kCustom, calls=%fused_computation.11.clone | custom fusion | bytes 6291488 | tf_op jit(solution)/shard_map/jit(_take)/gather | solution.py:68
  210.4 4.9 %gather_fusion.18 = bf16[8,768,256]{2,1,0:T(8,128)(2,1)} fusion(bf16[768,14,256]{2,0,1:T(8,128)(2,1)} %copy.46, s32[1024]{0:T(1024)S(1)} %pad_clamp_fusion.6), kind=kCustom, calls=%fused_computation.12.clone | custom fusion | bytes 6291488 | tf_op jit(solution)/shard_map/jit(_take)/gather | solution.py:68
  215.3 5.0 %gather_fusion.21 = bf16[8,768,256]{2,1,0:T(8,128)(2,1)} fusion(bf16[768,14,256]{2,0,1:T(8,128)(2,1)} %copy.46, s32[1024]{0:T(1024)S(1)} %pad_clamp_fusion.5), kind=kCustom, calls=%fused_computation.13.clone | custom fusion | bytes 6291488 | tf_op jit(solution)/shard_map/jit(_take)/gather | solution.py:68
  220.3 4.9 %gather_fusion.24 = bf16[8,768,256]{2,1,0:T(8,128)(2,1)} fusion(bf16[768,14,256]{2,0,1:T(8,128)(2,1)} %copy.46, s32[1024]{0:T(1024)S(1)} %pad_clamp_fusion.4), kind=kCustom, calls=%fused_computation.14.clone | custom fusion | bytes 6291488 | tf_op jit(solution)/shard_map/jit(_take)/gather | solution.py:68
  225.7 3.9 %fusion.181 = f32[8,256,32]{1,2,0:T(8,128)S(1)} fusion(bf16[8,768,256]{2,1,0:T(8,128)(2,1)} %gather_fusion.6, pred[8]{0:T(512)(128)(4,1)S(1)} %copy-done.8, f32[8,256]{1,0:T(8,128)S(1)} %add.371, f32[8,256]{1,0:T(8,128)S(1)} %broadcast_select_fusion.6, bf16[96,8,8,256]{3,2,1,0:T(8,128)(2,1)} %bitcast.278, bf16[8,32,256]{2,1,0:T(8,128)(2,1)S(1)} %gather_fusion.7, ...), kind=kOutput, calls=%fused_computation.117 | convolution fusion | flops 843186176 | bytes 6701072 | tf_op jit(solution)/shard_map/pia,iab->pib/dot_general | solution.py:73
  229.6 3.9 %fusion.176 = f32[8,256,32]{1,2,0:T(8,128)S(1)} fusion(f32[8,256,32]{1,2,0:T(8,128)S(1)} %fusion.181, bf16[8,768,256]{2,1,0:T(8,128)(2,1)} %gather_fusion.9, pred[8]{0:T(512)(128)(4,1)S(1)} %get-tuple-element.57, f32[8,256]{1,0:T(8,128)S(1)} %broadcast_select_fusion.5, f32[8,256]{1,0:T(8,128)S(1)} %add.371, bf16[96,8,8,256]{3,2,1,0:T(8,128)(2,1)} %bitcast.279, ...), kind=kOutput, calls=%fused_computation.116 | convolution fusion | flops 843251712 | bytes 6963216 | tf_op jit(solution)/shard_map/pia,iab->pib/dot_general | solution.py:73
  233.5 3.9 %fusion.166 = f32[8,256,32]{1,2,0:T(8,128)S(1)} fusion(f32[8,256,32]{1,2,0:T(8,128)S(1)} %fusion.176, bf16[8,768,256]{2,1,0:T(8,128)(2,1)} %gather_fusion.12, pred[8]{0:T(512)(128)(4,1)S(1)} %get-tuple-element.56, f32[8,256]{1,0:T(8,128)S(1)} %broadcast_select_fusion.4, f32[8,256]{1,0:T(8,128)S(1)} %add.371, bf16[96,8,8,256]{3,2,1,0:T(8,128)(2,1)} %bitcast.280, ...), kind=kOutput, calls=%fused_computation.114 | convolution fusion | flops 843251712 | bytes 6963216 | tf_op jit(solution)/shard_map/pia,iab->pib/dot_general | solution.py:73
  237.4 3.9 %fusion.156 = f32[8,256,32]{1,2,0:T(8,128)S(1)} fusion(f32[8,256,32]{1,2,0:T(8,128)S(1)} %fusion.166, bf16[8,768,256]{2,1,0:T(8,128)(2,1)} %gather_fusion.15, pred[8]{0:T(512)(128)(4,1)S(1)} %get-tuple-element.55, f32[8,256]{1,0:T(8,128)S(1)} %broadcast_select_fusion.3, f32[8,256]{1,0:T(8,128)S(1)} %add.371, bf16[96,8,8,256]{3,2,1,0:T(8,128)(2,1)} %bitcast.281, ...), kind=kOutput, calls=%fused_computation.112 | convolution fusion | flops 843251712 | bytes 6963216 | tf_op jit(solution)/shard_map/pia,iab->pib/dot_general | solution.py:73
  241.3 3.9 %fusion.146 = f32[8,256,32]{1,2,0:T(8,128)S(1)} fusion(f32[8,256,32]{1,2,0:T(8,128)S(1)} %fusion.156, bf16[8,768,256]{2,1,0:T(8,128)(2,1)} %gather_fusion.18, pred[8]{0:T(512)(128)(4,1)S(1)} %get-tuple-element.54, f32[8,256]{1,0:T(8,128)S(1)} %broadcast_select_fusion.2, f32[8,256]{1,0:T(8,128)S(1)} %add.371, bf16[96,8,8,256]{3,2,1,0:T(8,128)(2,1)} %bitcast.282, ...), kind=kOutput, calls=%fused_computation.110 | convolution fusion | flops 843251712 | bytes 6963216 | tf_op jit(solution)/shard_map/pia,iab->pib/dot_general | solution.py:73
  245.2 4.0 %fusion.136 = f32[8,256,32]{1,2,0:T(8,128)S(1)} fusion(f32[8,256,32]{1,2,0:T(8,128)S(1)} %fusion.146, bf16[8,768,256]{2,1,0:T(8,128)(2,1)} %gather_fusion.21, pred[8]{0:T(512)(128)(4,1)S(1)} %get-tuple-element.53, f32[8,256]{1,0:T(8,128)S(1)} %broadcast_select_fusion.1, f32[8,256]{1,0:T(8,128)S(1)} %add.371, bf16[96,8,8,256]{3,2,1,0:T(8,128)(2,1)} %bitcast.283, ...), kind=kOutput, calls=%fused_computation.108 | convolution fusion | flops 843251712 | bytes 6963216 | tf_op jit(solution)/shard_map/pia,iab->pib/dot_general | solution.py:73
  249.1 4.1 %fusion.126 = f32[8,4,8,256]{3,2,1,0:T(8,128)S(1)} fusion(f32[8,256,32]{1,2,0:T(8,128)S(1)} %fusion.136, bf16[8,768,256]{2,1,0:T(8,128)(2,1)} %gather_fusion.24, pred[8]{0:T(512)(128)(4,1)S(1)} %get-tuple-element.52, f32[8,256]{1,0:T(8,128)S(1)} %broadcast_select_fusion, f32[8,256]{1,0:T(8,128)S(1)} %add.371, bf16[96,8,8,256]{3,2,1,0:T(8,128)(2,1)} %bitcast.284, ...), kind=kOutput, calls=%fused_computation.106 | convolution fusion | flops 843251712 | bytes 6963216 | tf_op jit(solution)/shard_map/pia,iab->pib/dot_general | solution.py:73
  253.5 3.6 %reduce_sum.51 = f32[32,1920]{1,0:T(8,128)S(1)} reduce(f32[32,32,1920]{2,1,0:T(8,128)} %all-gather.4.cloned.1.call-done, f32[]{:T(128)} %constant.205.clone.1), dimensions={0}, to_apply=%region_3.7 | reduce | flops 1904640 | bytes 8110084 | tf_op jit(solution)/shard_map/reduce_sum | solution.py:137
  258.0 3.2 %fusion.44 = f32[2048,32]{0,1:T(8,128)S(1)} fusion(f32[32,2048]{1,0:T(8,128)S(1)} %bitcast.292, bf16[768,2048]{1,0:T(8,128)(2,1)} %param.13, f32[2048]{0:T(1024)S(1)} %multiply_reduce_fusion.1, f32[256]{0:T(256)S(1)} %multiply_reduce_fusion.2, bf16[768,64]{0,1:T(8,128)(2,1)S(1)} %get-tuple-element.28, bf16[768,64]{0,1:T(8,128)(2,1)S(1)} %get-tuple-element.30, ...), kind=kOutput, calls=%fused_computation.79 | convolution fusion | flops 843186176 | bytes 4088832 | tf_op jit(solution)/shard_map/dot_general | solution.py:151
  261.6 5.8 %scatter_custom_fusion = f32[32,2048]{0,1:T(8,128)S(1)} fusion(s32[2048]{0:T(1024)S(1)} %bitcast.294, f32[2048,32]{1,0:T(8,128)S(1)} %copy.80, f32[]{:T(128)} %constant.205.clone.1), kind=kCustom, calls=%fused_computation.168 | custom fusion | bytes 262148 | tf_op jit(solution)/shard_map/scatter | solution.py:155
  267.4 1.0 copy.81
  (86 shorter events, 7.0 us)
Async XLA Ops:
  6.5 250.6 %copy-start = (f32[30,64,64]{2,1,0:T(8,128)S(1)}, f32[30,64,64]{2,1,0:T(8,128)}, u32[]{:S(2)}) copy-start(f32[30,64,64]{2,1,0:T(8,128)} %param.19) | copy-start | bytes 1474564
  6.5 82.3 %all-gather.6.cloned.1.call-start = ((), (), s32[]{:S(2)}) async-start(), calls=%async_computation.1 | async-start | bytes 3244032 | tf_op jit(solution)/shard_map/all_gather | solution.py:103
  10.4 1.3 copy-start.6
  19.3 9.9 %copy-start.2 = (bf16[32,2048]{1,0:T(8,128)(2,1)S(1)}, bf16[32,2048]{1,0:T(8,128)(2,1)}, u32[]{:S(2)}) copy-start(bf16[32,2048]{1,0:T(8,128)(2,1)} %param.14) | copy-start | bytes 393220
  19.4 10.2 %copy-start.3 = (s32[1,2048]{1,0:T(1,128)S(1)}, s32[1,2048]{1,0:T(1,128)}, u32[]{:S(2)}) copy-start(s32[1,2048]{1,0:T(1,128)} %param.15) | copy-start | bytes 24580
  29.1 224.3 %all-gather.4.cloned.1.call-start = ((), (), s32[]{:S(2)}) async-start(), calls=%async_computation | async-start | bytes 8110080 | tf_op jit(solution)/shard_map/all_gather | solution.py:136
  113.0 0.7 copy-start.1
  116.6 9.9 %copy-start.4 = (s32[8]{0:T(128)S(1)}, s32[8]{0:T(128)}, u32[]{:S(2)}) copy-start(s32[8]{0:T(128)} %get-tuple-element.6) | copy-start | bytes 100
  116.6 9.9 %copy-start.5 = (s32[8]{0:T(128)S(1)}, s32[8]{0:T(128)}, u32[]{:S(2)}) copy-start(s32[8]{0:T(128)} %get-tuple-element.8) | copy-start | bytes 100
  116.6 10.0 %copy-start.7 = (s32[8]{0:T(128)S(1)}, s32[8]{0:T(128)}, u32[]{:S(2)}) copy-start(s32[8]{0:T(128)} %copy-done.6) | copy-start | bytes 100
  116.6 10.1 %copy-start.9 = (s32[1,8]{1,0:T(1,128)S(1)}, s32[1,8]{1,0:T(1,128)}, u32[]{:S(2)}) copy-start(s32[1,8]{1,0:T(1,128)} %param.17) | copy-start | bytes 100
  119.1 40.5 %collective-permute-start.1 = (bf16[800,768]{1,0:T(8,128)(2,1)}, bf16[800,768]{1,0:T(8,128)(2,1)}, u32[]{:S(2)}, u32[]{:S(2)}) collective-permute-start(bf16[800,768]{1,0:T(8,128)(2,1)} %copy.43), channel_id=1, source_target_pairs={{1,0},{2,1},{3,2},{4,3},{5,4},{6,5},{7,6},{8,7},{9,8},{10,9},{11,1... | collective-permute-start | bytes 3686408 | tf_op jit(solution)/shard_map/ppermute | solution.py:21
  122.8 38.6 %collective-permute-start = (bf16[800,768]{1,0:T(8,128)(2,1)}, bf16[800,768]{1,0:T(8,128)(2,1)}, u32[]{:S(2)}, u32[]{:S(2)}) collective-permute-start(bf16[800,768]{1,0:T(8,128)(2,1)} %copy.42), channel_id=1, source_target_pairs={{0,1},{1,2},{2,3},{3,4},{4,5},{5,6},{6,7},{7,8},{8,9},{9,10},{10,1... | collective-permute-start | bytes 3686408 | tf_op jit(solution)/shard_map/ppermute | solution.py:18
  220.3 5.3 %copy-start.8 = (pred[8]{0:T(512)(128)(4,1)S(1)}, pred[8]{0:T(512)(128)(4,1)}, u32[]{:S(2)}) copy-start(pred[8]{0:T(512)(128)(4,1)} %get-tuple-element.58) | copy-start | bytes 28
Sparse Core Ops, SparseCore 0:
  29.3 59.5 all-gather.5
  113.9 83.1 all-gather.3
